TPU v7x, 32 devices: a whole 2x2x4 slice. The times are simulated.
32 devices in a mesh: fsdp: 8 (over y, x, core), tp: 4 (over z).
Axes of the slice: x: 2, y: 2, z: 4, core: 2. Of those that a mesh axis runs over, the one named last changes fastest.
Arguments:
- residual: bfloat16 [4096, 2048], P(('fsdp', 'tp')), may hold values from -6 to 6
- norm_gain: bfloat16 [2048], P(('fsdp', 'tp')), may hold values from 0.099609375 to 1.8984375
- norm_shift: bfloat16 [2048], P(('fsdp', 'tp')), may hold values from -1.75 to 1.75
- qkv_weight: bfloat16 [3, 2048, 2048], P(None, 'fsdp', 'tp'), may hold values from -0.125 to 0.125
- qkv_bias: bfloat16 [3, 2048], P(None, ('tp', 'fsdp')), may hold values from -1.75 to 1.75
- dense_weight: bfloat16 [2048, 2048], P('tp', 'fsdp'), may hold values from -0.75 to 0.75
- dense_bias: bfloat16 [2048], P(('fsdp', 'tp')), may hold values from -1.75 to 1.75
- inner_weight: bfloat16 [2048, 8192], P('fsdp', 'tp'), may hold values from -0.125 to 0.125
- inner_bias: bfloat16 [8192], P(('tp', 'fsdp')), may hold values from -1.75 to 1.75
- outer_weight: bfloat16 [8192, 2048], P('tp', 'fsdp'), may hold values from -0.0625 to 0.0625
- outer_bias: bfloat16 [2048], P(('fsdp', 'tp')), may hold values from -1.75 to 1.75
- cotangent: bfloat16 [4096, 2048], P(('fsdp', 'tp')), may hold values from -6 to 6
- segment: int32 [4096], replicated, may hold values from 0 to 38, as said below
- ancestors: int32 [39, 3], replicated, may hold values from 0 to 38, as said below
- valid_slot: int32 [4096], replicated, may hold values from 0 to 1, as said below
Outputs:
- output: bfloat16 [4096, 2048], P(('fsdp', 'tp'))
- residual_grad: bfloat16 [4096, 2048], P(('fsdp', 'tp'))
- norm_gain_grad: float32 [2048], P(('fsdp', 'tp'))
- norm_shift_grad: float32 [2048], P(('fsdp', 'tp'))
- qkv_weight_grad: float32 [3, 2048, 2048], P(None, 'fsdp', 'tp')
- qkv_bias_grad: float32 [3, 2048], P(None, ('tp', 'fsdp'))
- dense_weight_grad: float32 [2048, 2048], P('tp', 'fsdp')
- dense_bias_grad: float32 [2048], P(('fsdp', 'tp'))
- inner_weight_grad: float32 [2048, 8192], P('fsdp', 'tp')
- inner_bias_grad: float32 [8192], P(('tp', 'fsdp'))
- outer_weight_grad: float32 [8192, 2048], P('tp', 'fsdp')
- outer_bias_grad: float32 [2048], P(('fsdp', 'tp'))
Inputs may be any that keep to these rules, and one draw needn't show every extreme that they name: Each of the 3 trees fills 1024 consecutive slots, in order of slots: a trunk of 640 slots, then four branches and eight leaves of 32 slots each, two leaves to a branch, each leaf after its branch; the slots of a segment are consecutive and carry its id; padding slots carry 0. `ancestors`: row s names the trunk, branch and leaf segment of the path that ends in segment s, repeating s where the path is shorter; each tree's segments name only that tree's segments. `valid_slot`: 1 on exactly the slots that trees fill, 0 on the other 1024 slots.
All inputs are finite; a program needn't handle non-finite values.
Results may differ from a plain program's by a relative error of at most 0.0098.
Values may be sent and summed in bfloat16 or wider, within the bound.
No kernel may reach another device: no remote copies, remote signals or barrier semaphores. Data moves between devices by JAX's collectives and lax.ppermute only.
A program may use at most 192 MiB of HBM per device.

v0:
```python
import jax
import jax.numpy as jnp
from jax import lax
from jax.sharding import PartitionSpec as P

HEAD_DIM = 64
ROTARY = 32
TREE_LEN = 1024
EPSILON = 1e-05


def passed_along(value, axis, steps):
    count = lax.axis_size(axis)
    initial, last = (max(0, -steps), min(count, count - steps))
    return lax.ppermute(value, axis, [(source, source + steps) for source in range(initial, last)])


def norm_rows(inputs_f, gain_f, shift_f):
    row_mean = jnp.mean(inputs_f, axis=-1, keepdims=True)
    centered = inputs_f - row_mean
    variance = jnp.mean(centered * centered, axis=-1, keepdims=True)
    return centered * lax.rsqrt(variance + EPSILON) * gain_f + shift_f


def tree_allowed(query_seg, query_slot, query_valid, key_seg, key_slot, key_valid, ancestors):
    seg_ids = jnp.arange(ancestors.shape[0], dtype=jnp.int32)
    onehot = (query_seg[:, None] == seg_ids[None, :]).astype(jnp.int32)
    path_ids = jnp.sum(onehot[:, :, None] * ancestors[None, :, :], axis=1)
    linked = (
        (key_seg[None, :] == path_ids[:, 0:1])
        | (key_seg[None, :] == path_ids[:, 1:2])
        | (key_seg[None, :] == path_ids[:, 2:3])
    )
    earlier = key_slot[None, :] <= query_slot[:, None]
    usable = (key_valid[None, :] == 1) & (query_valid[:, None] == 1)
    return linked & earlier & usable | (key_slot[None, :] == query_slot[:, None])


def rotate(tensor, positions, direction):
    half_rot = ROTARY // 2
    freq = 10000.0 ** (-(jnp.arange(half_rot, dtype=jnp.float32) * 2.0 / ROTARY))
    angle = direction * positions.astype(jnp.float32)[:, None] * freq[None, :]
    cosine = jnp.cos(angle)[:, None, :]
    sine = jnp.sin(angle)[:, None, :]
    first = tensor[..., :half_rot]
    second = tensor[..., half_rot:ROTARY]
    return jnp.concatenate(
        [first * cosine - second * sine, second * cosine + first * sine, tensor[..., ROTARY:]],
        axis=-1,
    )


def body(
    residual,
    norm_gain,
    norm_shift,
    qkv_weight,
    qkv_bias,
    dense_weight,
    dense_bias,
    inner_weight,
    inner_bias,
    outer_weight,
    outer_bias,
    cotangent,
    segment,
    ancestors,
    valid_slot,
):
    f32 = jnp.float32
    bf16 = jnp.bfloat16
    tp_size = lax.axis_size("tp")
    local_rows = residual.shape[0]
    group_rows = local_rows * tp_size
    head_cols = qkv_weight.shape[2]
    head_count = head_cols // HEAD_DIM
    reach_back = (TREE_LEN - 2) // group_rows + 1
    front_rows = reach_back * group_rows
    window = front_rows + group_rows
    block_rows = min(512, group_rows)
    block_count = group_rows // block_rows
    scaling = HEAD_DIM ** (-0.5)
    base_slot = lax.axis_index("fsdp") * group_rows
    vectors = (
        lax.all_gather(norm_gain, ("fsdp", "tp"), axis=0, tiled=True),
        lax.all_gather(norm_shift, ("fsdp", "tp"), axis=0, tiled=True),
        lax.all_gather(dense_bias, ("fsdp", "tp"), axis=0, tiled=True),
        lax.all_gather(outer_bias, ("fsdp", "tp"), axis=0, tiled=True),
    )
    gain_f = vectors[0].astype(f32)
    shift_f = vectors[1].astype(f32)
    bias_sum = vectors[2].astype(f32) + vectors[3].astype(f32)
    seg_front = jnp.concatenate([jnp.zeros((front_rows,), jnp.int32), segment])
    valid_front = jnp.concatenate([jnp.zeros((front_rows,), jnp.int32), valid_slot])
    query_slot = base_slot + jnp.arange(group_rows, dtype=jnp.int32)
    query_seg = lax.dynamic_slice_in_dim(segment, base_slot, group_rows)
    query_valid = lax.dynamic_slice_in_dim(valid_slot, base_slot, group_rows)
    key_slot = base_slot - front_rows + jnp.arange(window, dtype=jnp.int32)
    key_seg = lax.dynamic_slice_in_dim(seg_front, base_slot, window)
    key_valid = lax.dynamic_slice_in_dim(valid_front, base_slot, window)

    def allowed_for():
        return tree_allowed(
            query_seg, query_slot, query_valid, key_seg, key_slot, key_valid, ancestors
        )

    def count_keys(block_num):
        return jnp.sum(allowed_for().astype(jnp.int32), axis=1) - 1

    block_ids = jnp.arange(block_count, dtype=jnp.int32)
    positions = lax.map(count_keys, block_ids).reshape(group_rows)
    inputs_f = residual.astype(f32)
    normed_local = norm_rows(inputs_f, gain_f, shift_f).astype(bf16)

    def key_window(keys_own, values_own):
        key_parts = []
        value_parts = []
        for distance in range(reach_back, 0, -1):
            got_keys, got_values = passed_along((keys_own, values_own), "fsdp", distance)
            key_parts.append(got_keys)
            value_parts.append(got_values)
        return (
            jnp.concatenate(key_parts + [keys_own], axis=0),
            jnp.concatenate(value_parts + [values_own], axis=0),
        )

    def forward_pieces():
        gathered = (
            lax.all_gather(qkv_weight, "fsdp", axis=1, tiled=True),
            lax.all_gather(qkv_bias, "fsdp", axis=1, tiled=True),
            lax.all_gather(dense_weight, "fsdp", axis=1, tiled=True),
            lax.all_gather(inner_weight, "fsdp", axis=0, tiled=True),
            lax.all_gather(inner_bias, "fsdp", axis=0, tiled=True),
            lax.all_gather(outer_weight, "fsdp", axis=1, tiled=True),
        )
        normed = lax.all_gather(normed_local, "tp", axis=0, tiled=True)
        w_qkv = gathered[0]
        mixed = (
            jnp.einsum("td,sde->ste", normed, w_qkv, preferred_element_type=f32)
            + gathered[1].astype(f32)[:, None, :]
        )
        queries = rotate(mixed[0].reshape(group_rows, head_count, HEAD_DIM), positions, 1.0).astype(
            bf16
        )
        keys_own = (
            rotate(mixed[1].reshape(group_rows, head_count, HEAD_DIM), positions, 1.0)
            .astype(bf16)
            .reshape(group_rows, head_cols)
        )
        values_own = mixed[2].astype(bf16)
        keys_win, values_win = key_window(keys_own, values_own)
        keys_win = keys_win.reshape(window, head_count, HEAD_DIM)
        values_win = values_win.reshape(window, head_count, HEAD_DIM)

        def attend(block_num):
            scores = (
                jnp.einsum("qhe,khe->hqk", queries, keys_win, preferred_element_type=f32) * scaling
            )
            scores = jnp.where(allowed_for()[None], scores, -jnp.inf)
            top_score = jnp.max(scores, axis=-1, keepdims=True)
            expo = jnp.exp(scores - top_score)
            summed = jnp.sum(expo, axis=-1, keepdims=True)
            probs_low = (expo / summed).astype(bf16)
            attended = jnp.einsum("hqk,khe->qhe", probs_low, values_win, preferred_element_type=f32)
            return (attended, (top_score + jnp.log(summed))[..., 0])

        attended, log_sums = lax.map(attend, block_ids)
        attended = attended.reshape(group_rows, head_cols).astype(bf16)
        pre_act = jnp.dot(normed, gathered[3], preferred_element_type=f32) + gathered[4].astype(f32)
        activated = jax.nn.gelu(pre_act, approximate=True).astype(bf16)
        return (
            gathered,
            normed,
            queries,
            keys_win,
            values_win,
            attended,
            log_sums,
            pre_act,
            activated,
        )

    gathered, normed, queries, keys_win, values_win, attended, log_sums, pre_act, activated = (
        forward_pieces()
    )
    partial_rows = jnp.dot(attended, gathered[2], preferred_element_type=f32) + jnp.dot(
        activated, gathered[5], preferred_element_type=f32
    )
    summed_rows = lax.psum_scatter(partial_rows, "tp", scatter_dimension=0, tiled=True)
    output = (inputs_f + summed_rows + bias_sum).astype(bf16)
    out_bias_grad = jnp.sum(cotangent.astype(f32), axis=0)
    grad_rows = lax.all_gather(cotangent, "tp", axis=0, tiled=True)
    gathered, normed, queries, keys_win, values_win, attended, log_sums, pre_act, activated = (
        forward_pieces()
    )
    w_qkv = gathered[0]
    w_dense = gathered[2]
    w_inner = gathered[3]
    w_outer = gathered[5]
    outer_grad = jnp.einsum("tf,td->fd", activated, grad_rows, preferred_element_type=f32)
    act_grad = jnp.einsum("td,fd->tf", grad_rows, w_outer, preferred_element_type=f32)
    unused_value, gelu_pull = jax.vjp(
        lambda inputs_g: jax.nn.gelu(inputs_g, approximate=True), pre_act
    )
    pre_grad = gelu_pull(act_grad)[0].astype(bf16)
    inner_grad = jnp.einsum("td,tf->df", normed, pre_grad, preferred_element_type=f32)
    inner_bias_grad = jnp.sum(pre_grad.astype(f32), axis=0)
    normed_grad = jnp.einsum("tf,df->td", pre_grad, w_inner, preferred_element_type=f32)
    dense_grad = jnp.einsum("tc,td->cd", attended, grad_rows, preferred_element_type=f32)
    attn_grad = (
        jnp.einsum("td,cd->tc", grad_rows, w_dense, preferred_element_type=f32)
        .astype(bf16)
        .reshape(group_rows, head_count, HEAD_DIM)
    )

    def attend_back(carry, inputs_b):
        key_acc, value_acc = carry
        block_num, log_block = inputs_b
        scores = jnp.einsum("qhe,khe->hqk", queries, keys_win, preferred_element_type=f32) * scaling
        probs = jnp.where(allowed_for()[None], jnp.exp(scores - log_block[..., None]), 0.0)
        probs_low = probs.astype(bf16)
        prob_grad = jnp.einsum("qhe,khe->hqk", attn_grad, values_win, preferred_element_type=f32)
        row_dot = jnp.sum(probs * prob_grad, axis=-1, keepdims=True)
        score_grad = (probs * (prob_grad - row_dot)).astype(bf16)
        query_grad = (
            jnp.einsum("hqk,khe->qhe", score_grad, keys_win, preferred_element_type=f32) * scaling
        )
        key_part = (
            key_acc
            + jnp.einsum("hqk,qhe->khe", score_grad, queries, preferred_element_type=f32) * scaling
        )
        value_part = value_acc + jnp.einsum(
            "hqk,qhe->khe", probs_low, attn_grad, preferred_element_type=f32
        )
        key_acc = key_part
        value_acc = value_part
        return ((key_acc, value_acc), query_grad)

    zero_window = jnp.zeros((window, head_count, HEAD_DIM), f32)
    (key_acc, value_acc), query_grads = lax.scan(
        attend_back, (zero_window, zero_window), (block_ids, log_sums)
    )
    key_flat = key_acc.reshape(window, head_cols)
    value_flat = value_acc.reshape(window, head_cols)
    own_key = key_flat[front_rows:]
    own_value = value_flat[front_rows:]
    for distance in range(1, reach_back + 1):
        lower = front_rows - distance * group_rows
        got_key, got_value = passed_along(
            (key_flat[lower : lower + group_rows], value_flat[lower : lower + group_rows]),
            "fsdp",
            -distance,
        )
        own_key = own_key + got_key
        own_value = own_value + got_value
    query_pre = rotate(
        query_grads.reshape(group_rows, head_count, HEAD_DIM), positions, -1.0
    ).reshape(group_rows, head_cols)
    key_pre = rotate(own_key.reshape(group_rows, head_count, HEAD_DIM), positions, -1.0).reshape(
        group_rows, head_cols
    )
    qkv_grad = jnp.stack([query_pre, key_pre, own_value]).astype(bf16)
    qkv_weight_part = jnp.einsum("td,ste->sde", normed, qkv_grad, preferred_element_type=f32)
    qkv_bias_part = jnp.sum(qkv_grad.astype(f32), axis=1)
    normed_grad = normed_grad + jnp.einsum(
        "ste,sde->td", qkv_grad, w_qkv, preferred_element_type=f32
    )
    local_grad = lax.psum_scatter(normed_grad, "tp", scatter_dimension=0, tiled=True)
    unused_norm, norm_pull = jax.vjp(norm_rows, inputs_f, gain_f, shift_f)
    input_grad, gain_grad, shift_grad = norm_pull(local_grad)
    residual_grad = (cotangent.astype(f32) + input_grad).astype(bf16)
    weight_sums = (
        lax.psum_scatter(qkv_weight_part, "fsdp", scatter_dimension=1, tiled=True),
        lax.psum_scatter(qkv_bias_part, "fsdp", scatter_dimension=1, tiled=True),
        lax.psum_scatter(dense_grad, "fsdp", scatter_dimension=1, tiled=True),
        lax.psum_scatter(inner_grad, "fsdp", scatter_dimension=0, tiled=True),
        lax.psum_scatter(inner_bias_grad, "fsdp", scatter_dimension=0, tiled=True),
        lax.psum_scatter(outer_grad, "fsdp", scatter_dimension=1, tiled=True),
    )
    vector_sums = (
        lax.psum_scatter(gain_grad, ("fsdp", "tp"), scatter_dimension=0, tiled=True),
        lax.psum_scatter(shift_grad, ("fsdp", "tp"), scatter_dimension=0, tiled=True),
        lax.psum_scatter(out_bias_grad, ("fsdp", "tp"), scatter_dimension=0, tiled=True),
    )
    return (
        output,
        residual_grad,
        vector_sums[0],
        vector_sums[1],
        weight_sums[0],
        weight_sums[1],
        weight_sums[2],
        vector_sums[2],
        weight_sums[3],
        weight_sums[4],
        weight_sums[5],
        vector_sums[2],
    )


def solution(mesh):
    return jax.shard_map(
        body,
        mesh=mesh,
        in_specs=(
            P(("fsdp", "tp"), None),
            P(("fsdp", "tp")),
            P(("fsdp", "tp")),
            P(None, "fsdp", "tp"),
            P(None, ("tp", "fsdp")),
            P("tp", "fsdp"),
            P(("fsdp", "tp")),
            P("fsdp", "tp"),
            P(("tp", "fsdp")),
            P("tp", "fsdp"),
            P(("fsdp", "tp")),
            P(("fsdp", "tp"), None),
            P(),
            P(),
            P(),
        ),
        out_specs=(
            P(("fsdp", "tp"), None),
            P(("fsdp", "tp"), None),
            P(("fsdp", "tp")),
            P(("fsdp", "tp")),
            P(None, "fsdp", "tp"),
            P(None, ("tp", "fsdp")),
            P("tp", "fsdp"),
            P(("fsdp", "tp")),
            P("fsdp", "tp"),
            P(("tp", "fsdp")),
            P("tp", "fsdp"),
            P(("fsdp", "tp")),
        ),
        check_vma=False,
    )
```

profile of v0, /device:TPU:0, one launch (start us, length us, event | category | flops | bytes accessed | tf_op | source)
XLA Modules:
  0.0 1016.9 jit_solution(10757736382496534110)
XLA Ops:
  10.7 42.2 %all-reduce.11 = (bf16[2048]{0:T(1024)(128)(2,1)S(1)}, bf16[2048]{0:T(1024)(128)(2,1)S(1)}, bf16[2048]{0:T(1024)(128)(2,1)}, bf16[2048]{0:T(1024)(128)(2,1)}) all-reduce(bf16[2048]{0:T(1024)(128)(2,1)S(1)} %dynamic-update-slice.1, bf16[2048]{0:T(1024)(128)(2,1)S(1)} %dynamic-update-slice, ...), channel_id=1, replica_groups=mesh['fsdp'=8,'tp'=4] {'fsdp','tp'}, use_global_device_ids=true, to_apply=%add.3 | all-reduce | flops 8192 | bytes 32768
  56.0 2.2 fusion.31
  58.3 2.3 copy.69
  63.7 1.9 convert_reduce_fusion.2
  65.6 10.2 %all-gather = bf16[8,64,3]{1,2,0:T(4,128)(2,1)S(1)} all-gather(bf16[1,64,3]{1,2,0:T(4,128)(2,1)S(1)} %bitcast.110), channel_id=1, replica_groups=mesh['fsdp'=8,'tp'=4] {'fsdp'}, dimensions={0}, use_global_device_ids=true | all-gather | bytes 3456 | tf_op jit(solution)/shard_map/all_gather | solution.py:130
  75.9 7.9 all-gather.1
  85.4 19.4 %all-gather.9.cloned.1.call-done = bf16[512,2048]{1,0:T(8,128)(2,1)} async-done(((bf16[128,2048]{1,0:T(8,128)(2,1)}), bf16[512,2048]{1,0:T(8,128)(2,1)}) %all-gather.9.cloned.1.call-update) | async-done | bytes 2097168 | tf_op jit(solution)/shard_map/all_gather | solution.py:136
  104.8 47.9 %all-gather.11.cloned.1.call-done = bf16[3,2048,512]{1,2,0:T(8,128)(2,1)} async-done(((bf16[3,256,512]{1,2,0:T(8,128)(2,1)}), bf16[3,2048,512]{1,2,0:T(8,128)(2,1)}) %all-gather.11.cloned.1.call-update) | async-done | bytes 6291472 | tf_op jit(solution)/shard_map/all_gather | solution.py:129
  152.6 6.2 add_bitcast_fusion
  160.6 4.2 collective-permute-start.2
  164.7 2.7 collective-permute-start.3
  167.4 32.8 %all-gather.19.cloned.1.call-done = bf16[512,2048]{1,0:T(8,128)(2,1)} async-done(((bf16[128,2048]{1,0:T(8,128)(2,1)}), bf16[512,2048]{1,0:T(8,128)(2,1)}) %all-gather.19.cloned.1.call-update) | async-done | bytes 2097168 | tf_op jit(solution)/shard_map/all_gather | solution.py:192
  200.2 28.7 %all-gather.13.cloned.1.call-done = bf16[512,2048]{1,0:T(8,128)(2,1)} async-done(((bf16[512,256]{1,0:T(8,128)(2,1)}), bf16[512,2048]{1,0:T(8,128)(2,1)}) %all-gather.13.cloned.1.call-update) | async-done | bytes 2097168 | tf_op jit(solution)/shard_map/all_gather | solution.py:131
  228.9 3.5 convolution_convert_fusion
  233.8 3.4 collective-permute-start
  237.2 2.2 collective-permute-start.1
  239.4 11.9 %select_reduce_fusion = (f32[8,512]{1,0:T(8,128)S(1)}, f32[8,512,1536]{2,1,0:T(8,128)}) fusion(pred[512,1536]{1,0:T(8,128)(4,1)S(1)} %get-tuple-element.236, bf16[512,8,64]{0,2,1:T(8,128)(2,1)S(1)} %maximum_convert_fusion, bf16[512,8,64]{0,2,1:T(8,128)(2,1)} %bitcast.14, bf16[512,8,64]{0,2,1:T(8,128)(2,1)} %bitcast.13, bf16[512,8,32]{0,2,1:T(8,128)(2,1)S(1)} %slice.202, ...), kind=kOutput, calls=%fused_computation.5 | convolution fusion | flops 830468096 | bytes 28065792 | tf_op jit(solution)/shard_map/while/body/eval_jaxpr/qhe,khe->hqk/dot_general | solution.py:157
  251.3 11.6 %fusion = f32[8,512]{1,0:T(8,128)S(1)} fusion(f32[8,512,1536]{2,1,0:T(8,128)} %get-tuple-element.268, f32[8,512]{1,0:T(8,128)S(1)} %get-tuple-element.267, pred[512,1536]{1,0:T(8,128)(4,1)S(1)} %get-tuple-element.236), kind=kLoop, calls=%fused_computation.6 | loop fusion | flops 25161728 | bytes 25985024 | tf_op jit(solution)/shard_map/while/body/eval_jaxpr/reduce_sum | solution.py:162
  263.5 19.6 %multiply_reduce_fusion = (f32[8,512]{1,0:T(8,128)S(1)}, f32[8,512,1536]{2,1,0:T(8,128)}) fusion(f32[8,512,1536]{2,1,0:T(8,128)} %get-tuple-element.268, f32[8,512]{1,0:T(8,128)S(1)} %log_add_fusion, pred[512,1536]{1,0:T(8,128)(4,1)S(1)} %get-tuple-element.236, bf16[512,8,64]{0,2,1:T(8,128)(2,1)S(1)} %bitcast.100, bf16[1536,8,64]{0,2,1:T(8,128)(2,1)S(1)} %bitcast.82), kind=kOutput, calls=%fused_computation.1 | convolution fusion | flops 836759552 | bytes 53248000 | tf_op jit(solution)/shard_map/while/body/eval_jaxpr/qhe,khe->hqk/dot_general | solution.py:222
  283.1 17.4 %multiply_convert_fusion = bf16[8,512,1536]{2,1,0:T(8,128)(2,1)S(1)} fusion(f32[8,512,1536]{2,1,0:T(8,128)} %get-tuple-element.270, f32[8,512,1536]{2,1,0:T(8,128)} %get-tuple-element.268, f32[8,512]{1,0:T(8,128)S(1)} %get-tuple-element.269, f32[8,512]{1,0:T(8,128)S(1)} %log_add_fusion, pred[512,1536]{1,0:T(8,128)(4,1)S(1)} %get-tuple-element.236), kind=kLoop, calls=%fused_computation | loop fusion | flops 37748736 | bytes 63733760 | tf_op jit(solution)/shard_map/while/body/eval_jaxpr/convert_element_type | solution.py:224
  300.5 2.3 fusion.13
  302.8 2.7 copy-done
  305.4 1.8 fusion.57
  309.8 10.9 %fusion.14 = f32[1536,8,64]{0,2,1:T(8,128)S(1)} fusion(bf16[512,8,64]{0,2,1:T(8,128)(2,1)S(1)} %bitcast.101, f32[8,512,1536]{2,1,0:T(8,128)} %get-tuple-element.268, f32[8,512]{1,0:T(8,128)S(1)} %log_add_fusion, pred[512,1536]{1,0:T(8,128)(4,1)S(1)} %get-tuple-element.236), kind=kOutput, calls=%fused_computation.26 | convolution fusion | flops 830472192 | bytes 29638656 | tf_op jit(solution)/shard_map/while/body/eval_jaxpr/hqk,qhe->khe/dot_general | solution.py:232
  320.7 1.6 fusion.58
  322.3 2.5 copy.71
  328.8 9.0 fusion.26
  338.8 1.6 copy.72
  340.4 22.6 %collective-permute-done.5 = f32[512,512]{0,1:T(8,128)} collective-permute-done((f32[512,512]{0,1:T(8,128)}, f32[512,512]{0,1:T(8,128)}, u32[]{:S(2)}, u32[]{:S(2)}) %collective-permute-start.5) | collective-permute-done | bytes 1048608 | tf_op jit(solution)/shard_map/ppermute | solution.py:15
  363.0 2.2 fusion.38
  366.0 1.6 subtract_convert_fusion.1
  368.4 2.0 copy.74
  370.4 1.8 pad_maximum_fusion.7
  372.2 2.0 copy.75
  374.3 11.8 %collective-permute-done.7 = f32[512,512]{1,0:T(8,128)} collective-permute-done((f32[512,512]{1,0:T(8,128)}, f32[512,512]{1,0:T(8,128)}, u32[]{:S(2)}, u32[]{:S(2)}) %collective-permute-start.7) | collective-permute-done | bytes 1048608 | tf_op jit(solution)/shard_map/ppermute | solution.py:15
  386.1 1.8 fusion.40
  388.7 1.4 convert_reduce_fusion.1
  391.0 8.8 reduce-scatter.12.cloned.1.call-start
  399.8 10.5 %fusion.61 = f32[512,2048]{1,0:T(8,128)} fusion(bf16[512,2048]{1,0:T(8,128)(2,1)} %all-gather.9.cloned.1.call-done, bf16[2048,2048]{1,0:T(8,128)(2,1)} %all-gather.15.cloned.1.call-done), kind=kOutput, calls=%fused_computation.123 | convolution fusion | flops 4294967296 | bytes 14680064 | tf_op jit(solution)/shard_map/dot_general | solution.py:169
  410.4 9.8 all-gather.17.cloned.1.call-done
  420.2 12.2 %convert_reduce_fusion = (f32[2048]{0:T(1024)S(1)}, bf16[512,2048]{1,0:T(8,128)(2,1)S(1)}) fusion(f32[512,2048]{1,0:T(8,128)} %fusion.61, f32[2048]{0:T(1024)S(1)} %bitcast.106, bf16[512,2048]{1,0:T(8,128)(2,1)} %all-gather.19.cloned.1.call-done, bf16[2048,2048]{1,0:T(8,128)(2,1)} %all-gather.17.cloned.1.call-done), kind=kOutput, calls=%fused_computation.22 | convolution fusion | flops 4319082496 | bytes 16793600 | tf_op jit(solution)/shard_map/td,fd->tf/dot_general | solution.py:201
  432.5 4.8 fusion.62
  437.3 7.9 bitcast_add_fusion
  446.0 11.6 %fusion.27 = bf16[8,64,512]{2,1,0:T(8,128)(2,1)S(1)} fusion(bf16[1536,8,64]{0,2,1:T(8,128)(2,1)S(1)} %bitcast.83, f32[8,512,1536]{2,1,0:T(8,128)} %get-tuple-element.268, f32[8,512]{1,0:T(8,128)S(1)} %copy-done.19, f32[8,512]{1,0:T(8,128)S(1)} %get-tuple-element.267, pred[512,1536]{1,0:T(8,128)(4,1)S(1)} %get-tuple-element.236), kind=kOutput, calls=%fused_computation.51 | convolution fusion | flops 837025792 | bytes 28082176 | tf_op jit(solution)/shard_map/while/body/eval_jaxpr/hqk,khe->qhe/dot_general | solution.py:164
  457.6 8.1 fusion.54
  465.7 3.4 convolution_add_fusion
  470.3 8.0 convolution_bitcast_fusion
  478.4 1.5 copy-done.11
  479.9 3.3 fusion.63
  483.5 12.6 %fusion.64 = f32[2048,2048]{1,0:T(8,128)} fusion(bf16[512,2048]{1,0:T(8,128)(2,1)} %all-gather.9.cloned.1.call-done, bf16[512,2048]{1,0:T(8,128)(2,1)} %copy-done.37), kind=kOutput, calls=%fused_computation.126 | convolution fusion | flops 4294967296 | bytes 20971520 | tf_op jit(solution)/shard_map/td,tf->df/dot_general | solution.py:206
  496.1 11.9 %fusion.53 = f32[2048,2048]{1,0:T(8,128)} fusion(bf16[512,2048]{1,0:T(8,128)(2,1)S(1)} %copy-done.11, f32[512,2048]{1,0:T(8,128)} %fusion.61, f32[2048]{0:T(1024)S(1)} %bitcast.108), kind=kOutput, calls=%fused_computation.116 | convolution fusion | flops 4305453056 | bytes 23076864 | tf_op jit(solution)/shard_map/tf,td->fd/dot_general | solution.py:200
  509.9 1.4 copy.82
  511.4 14.1 %all-reduce.9 = f32[2048]{0:T(1024)S(1)} all-reduce(f32[2048]{0:T(1024)S(1)} %get-tuple-element.233), channel_id=11, replica_groups=mesh['fsdp'=8,'tp'=4] {'fsdp'}, use_global_device_ids=true, to_apply=%region_23.24.clone | all-reduce | flops 2048 | bytes 16384
  526.1 10.6 %reduce-scatter.12.cloned.1.call-done = f32[128,2048]{1,0:T(8,128)} async-done(((f32[512,2048]{1,0:T(8,128)}), f32[128,2048]{1,0:T(8,128)}) %reduce-scatter.12.cloned.1.call-update) | async-done | bytes 1048592 | tf_op jit(solution)/shard_map/reduce_scatter | solution.py:268
  536.7 1.6 fusion.55
  538.3 1.7 fusion.32
  540.0 76.3 %reduce-scatter.10.cloned.1.call-done = f32[128,2048]{1,0:T(8,128)} async-done(((f32[512,2048]{1,0:T(8,128)}), f32[128,2048]{1,0:T(8,128)}) %reduce-scatter.10.cloned.1.call-update) | async-done | bytes 1048592 | tf_op jit(solution)/shard_map/reduce_scatter | solution.py:189
  616.3 3.2 convert_reduce_fusion.4
  619.5 41.2 %all-reduce.10 = (f32[2048]{0:T(1024)S(1)}, f32[2048]{0:T(1024)S(1)}, f32[2048]{0:T(1024)S(1)}) all-reduce(f32[2048]{0:T(1024)S(1)} %get-tuple-element.222, f32[2048]{0:T(1024)S(1)} %get-tuple-element.224, f32[2048]{0:T(1024)S(1)} %get-tuple-element.253), channel_id=4, replica_groups=mesh['fsdp'=8,'tp'=4] {'fsdp','tp'}, use_global_device_ids=true, to_apply=%region_12.13.clone | all-reduce | flops 6144 | bytes 49152
  661.9 51.6 %reduce-scatter.14.cloned.1.call-done = f32[3,256,512]{1,2,0:T(8,128)} async-done(((f32[3,2048,512]{1,2,0:T(8,128)}), f32[3,256,512]{1,2,0:T(8,128)}) %reduce-scatter.14.cloned.1.call-update) | async-done | bytes 1572880 | tf_op jit(solution)/shard_map/reduce_scatter | solution.py:273
  713.6 3.0 copy.78
  716.6 52.6 %reduce-scatter.16.cloned.1.call-done = f32[512,256]{1,0:T(8,128)} async-done(((f32[512,2048]{1,0:T(8,128)}), f32[512,256]{1,0:T(8,128)}) %reduce-scatter.16.cloned.1.call-update) | async-done | bytes 524304 | tf_op jit(solution)/shard_map/reduce_scatter | solution.py:275
  769.2 120.0 %reduce-scatter.18.cloned.1.call-done = f32[256,2048]{1,0:T(8,128)} async-done(((f32[2048,2048]{1,0:T(8,128)}), f32[256,2048]{1,0:T(8,128)}) %reduce-scatter.18.cloned.1.call-update) | async-done | bytes 2097168 | tf_op jit(solution)/shard_map/reduce_scatter | solution.py:276
  889.2 120.2 %reduce-scatter.20.cloned.1.call-done = f32[2048,256]{1,0:T(8,128)} async-done(((f32[2048,2048]{1,0:T(8,128)}), f32[2048,256]{1,0:T(8,128)}) %reduce-scatter.20.cloned.1.call-update) | async-done | bytes 2097168 | tf_op jit(solution)/shard_map/reduce_scatter | solution.py:278
  (166 shorter events, 31.5 us)
Async XLA Ops:
  7.2 56.0 %copy-start.21 = (s32[4096]{0:T(1024)S(1)}, s32[4096]{0:T(1024)}, u32[]{:S(2)}) copy-start(s32[4096]{0:T(1024)} %param.27) | copy-start | bytes 49156
  7.2 56.1 %copy-start.20 = (s32[4096]{0:T(1024)S(1)}, s32[4096]{0:T(1024)}, u32[]{:S(2)}) copy-start(s32[4096]{0:T(1024)} %param.29) | copy-start | bytes 49156
  7.2 56.3 %copy-start.29 = (s32[39,3]{0,1:T(4,128)S(1)}, s32[39,3]{0,1:T(4,128)}, u32[]{:S(2)}) copy-start(s32[39,3]{0,1:T(4,128)} %param.28) | copy-start | bytes 1408
  7.2 97.6 %all-gather.9.cloned.1.call-start = ((), (), s32[]{:S(2)}) async-start(), calls=%async_computation.7 | async-start | bytes 2621440 | tf_op jit(solution)/shard_map/all_gather | solution.py:136
  52.9 2.6 copy-start.16
  54.1 1.4 copy-start.22
  54.1 11.5 %copy-start.30 = (bf16[3,64]{1,0:T(4,128)(2,1)S(1)}, bf16[3,64]{1,0:T(4,128)(2,1)}, u32[]{:S(2)}) copy-start(bf16[3,64]{1,0:T(4,128)(2,1)} %param.19) | copy-start | bytes 1156
  54.1 21.8 %copy-start.34 = (bf16[256]{0:T(256)(128)(2,1)S(1)}, bf16[256]{0:T(256)(128)(2,1)}, u32[]{:S(2)}) copy-start(bf16[256]{0:T(256)(128)(2,1)} %param.23) | copy-start | bytes 1540
  55.5 8.2 copy-start.31
  55.5 0.5 copy-start.25
  58.3 94.3 %all-gather.11.cloned.1.call-start = ((), (), s32[]{:S(2)}) async-start(), calls=%async_computation.8 | async-start | bytes 7077888 | tf_op jit(solution)/shard_map/all_gather | solution.py:129
  60.7 139.5 %all-gather.19.cloned.1.call-start = ((), (), s32[]{:S(2)}) async-start(), calls=%async_computation.13 | async-start | bytes 2621440 | tf_op jit(solution)/shard_map/all_gather | solution.py:192
  61.4 167.5 %all-gather.13.cloned.1.call-start = ((), (), s32[]{:S(2)}) async-start(), calls=%async_computation.9 | async-start | bytes 2359296 | tf_op jit(solution)/shard_map/all_gather | solution.py:131
  62.0 337.9 %all-gather.15.cloned.1.call-start = ((), (), s32[]{:S(2)}) async-start(), calls=%async_computation.10 | async-start | bytes 9437184 | tf_op jit(solution)/shard_map/all_gather | solution.py:132
  62.6 357.7 %all-gather.17.cloned.1.call-start = ((), (), s32[]{:S(2)}) async-start(), calls=%async_computation.11 | async-start | bytes 9437184 | tf_op jit(solution)/shard_map/all_gather | solution.py:134
  63.1 446.8 %reduce-scatter.22.cloned.1.call-start = ((), (), s32[]{:S(2)}) async-start(), calls=%async_computation.19 | async-start | bytes 294912
  158.9 1.6 copy-start.4
  160.5 78.9 %copy-start.14 = (bf16[512,8,64]{0,2,1:T(8,128)(2,1)}, bf16[512,8,64]{0,2,1:T(8,128)(2,1)S(1)}, u32[]{:S(2)}) copy-start(bf16[512,8,64]{0,2,1:T(8,128)(2,1)S(1)} %maximum_convert_fusion) | copy-start | bytes 1572868
  160.6 78.8 %collective-permute-start.2 = (bf16[512,512]{0,1:T(8,128)(2,1)S(1)}, bf16[512,512]{0,1:T(8,128)(2,1)}, u32[]{:S(2)}, u32[]{:S(2)}) collective-permute-start(bf16[512,512]{0,1:T(8,128)(2,1)S(1)} %bitcast.97), channel_id=1, source_target_pairs={{0,8},{4,12},{8,16},{12,20},{16,24},{20,28},{1,9},{5,13},{9,17},{1... | collective-permute-start | bytes 1572872 | tf_op jit(solution)/shard_map/ppermute | solution.py:15
  164.7 74.7 %collective-permute-start.3 = (bf16[512,512]{0,1:T(8,128)(2,1)S(1)}, bf16[512,512]{0,1:T(8,128)(2,1)}, u32[]{:S(2)}, u32[]{:S(2)}) collective-permute-start(bf16[512,512]{0,1:T(8,128)(2,1)S(1)} %bitcast.98), channel_id=1, source_target_pairs={{0,4},{4,8},{8,12},{12,16},{16,20},{20,24},{24,28},{1,5},{5,9},{9,... | collective-permute-start | bytes 1572872 | tf_op jit(solution)/shard_map/ppermute | solution.py:15
  233.8 29.2 %collective-permute-start = (bf16[512,512]{0,1:T(8,128)(2,1)S(1)}, bf16[512,512]{0,1:T(8,128)(2,1)S(1)}, u32[]{:S(2)}, u32[]{:S(2)}) collective-permute-start(bf16[512,512]{0,1:T(8,128)(2,1)S(1)} %fusion.41), channel_id=1, source_target_pairs={{0,8},{4,12},{8,16},{12,20},{16,24},{20,28},{1,9},{5,13},{9,17},{1... | collective-permute-start | bytes 1572872 | tf_op jit(solution)/shard_map/ppermute | solution.py:15
  237.2 25.8 %collective-permute-start.1 = (bf16[512,512]{0,1:T(8,128)(2,1)S(1)}, bf16[512,512]{0,1:T(8,128)(2,1)S(1)}, u32[]{:S(2)}, u32[]{:S(2)}) collective-permute-start(bf16[512,512]{0,1:T(8,128)(2,1)S(1)} %fusion.41), channel_id=1, source_target_pairs={{0,4},{4,8},{8,12},{12,16},{16,20},{20,24},{24,28},{1,5},{5,9},{9,... | collective-permute-start | bytes 1572872 | tf_op jit(solution)/shard_map/ppermute | solution.py:15
  262.9 0.6 copy-start.18
  300.5 5.0 copy-start
  307.2 33.2 %collective-permute-start.4 = (f32[512,512]{0,1:T(8,128)}, f32[512,512]{0,1:T(8,128)}, u32[]{:S(2)}, u32[]{:S(2)}) collective-permute-start(f32[512,512]{0,1:T(8,128)} %bitcast.23), channel_id=1, source_target_pairs={{4,0},{8,4},{12,8},{16,12},{20,16},{24,20},{28,24},{5,1},{9,5},{13... | collective-permute-start | bytes 3145736 | tf_op jit(solution)/shard_map/ppermute | solution.py:15
  308.5 54.5 %collective-permute-start.5 = (f32[512,512]{0,1:T(8,128)}, f32[512,512]{0,1:T(8,128)}, u32[]{:S(2)}, u32[]{:S(2)}) collective-permute-start(f32[512,512]{0,1:T(8,128)} %bitcast.24), channel_id=1, source_target_pairs={{8,0},{12,4},{16,8},{20,12},{24,16},{28,20},{9,1},{13,5},{17,9},{2... | collective-permute-start | bytes 3145736 | tf_op jit(solution)/shard_map/ppermute | solution.py:15
  324.9 49.4 %collective-permute-start.6 = (f32[512,512]{1,0:T(8,128)}, f32[512,512]{1,0:T(8,128)}, u32[]{:S(2)}, u32[]{:S(2)}) collective-permute-start(f32[512,512]{1,0:T(8,128)} %copy.71), channel_id=1, source_target_pairs={{4,0},{8,4},{12,8},{16,12},{20,16},{24,20},{28,24},{5,1},{9,5},{13... | collective-permute-start | bytes 3145736 | tf_op jit(solution)/shard_map/ppermute | solution.py:15
  327.5 58.6 %collective-permute-start.7 = (f32[512,512]{1,0:T(8,128)}, f32[512,512]{1,0:T(8,128)}, u32[]{:S(2)}, u32[]{:S(2)}) collective-permute-start(f32[512,512]{1,0:T(8,128)} %copy.73), channel_id=1, source_target_pairs={{8,0},{12,4},{16,8},{20,12},{24,16},{28,20},{9,1},{13,5},{17,9},{2... | collective-permute-start | bytes 3145736 | tf_op jit(solution)/shard_map/ppermute | solution.py:15
  337.7 1.1 copy-start.2
  340.4 25.6 %copy-start.3 = (f32[512,8,64]{0,2,1:T(8,128)S(1)}, f32[512,8,64]{0,2,1:T(8,128)}, u32[]{:S(2)}) copy-start(f32[512,8,64]{0,2,1:T(8,128)} %copy-done.2) | copy-start | bytes 3145732
  340.4 27.2 %copy-start.15 = (bf16[512,8,32]{0,2,1:T(8,128)(2,1)S(1)}, bf16[512,8,32]{0,2,1:T(8,128)(2,1)}, u32[]{:S(2)}) copy-start(bf16[512,8,32]{0,2,1:T(8,128)(2,1)} %slice.201) | copy-start | bytes 786436
  387.9 0.8 copy-start.5
  391.0 29.2 %copy-start.24 = (f32[8,1,256]{2,1,0:T(1,128)S(1)}, f32[8,1,256]{2,1,0:T(1,128)}, u32[]{:S(2)}) copy-start(f32[8,1,256]{2,1,0:T(1,128)} %convert_element_type.155) | copy-start | bytes 24580
  391.0 145.7 %reduce-scatter.12.cloned.1.call-start = ((), (), s32[]{:S(2)}) async-start(), calls=%async_computation.14 | async-start | bytes 5242880 | tf_op jit(solution)/shard_map/reduce_scatter | solution.py:268
  420.2 12.3 %copy-start.33 = (bf16[2048,2048]{1,0:T(8,128)(2,1)S(1)}, bf16[2048,2048]{1,0:T(8,128)(2,1)}, u32[]{:S(2)}) copy-start(bf16[2048,2048]{1,0:T(8,128)(2,1)} %all-gather.15.cloned.1.call-done) | copy-start | bytes 25165828
  432.5 4.8 copy-start.37
  432.5 4.8 copy-start.6
  432.5 4.8 copy-start.7
  432.5 4.8 copy-start.9
  445.2 0.7 copy-start.19
  445.3 171.0 %reduce-scatter.10.cloned.1.call-start = ((), (), s32[]{:S(2)}) async-start(), calls=%async_computation.12 | async-start | bytes 5242880 | tf_op jit(solution)/shard_map/reduce_scatter | solution.py:189
  446.0 11.6 %copy-start.38 = (f32[512,2048]{1,0:T(8,128)S(1)}, f32[512,2048]{1,0:T(8,128)}, u32[]{:S(2)}) copy-start(f32[512,2048]{1,0:T(8,128)} %fusion.61) | copy-start | bytes 12582916
  457.6 8.1 copy-start.13
  469.1 1.0 copy-start.8
  469.1 1.2 copy-start.10
  469.1 244.5 %reduce-scatter.14.cloned.1.call-start = ((), (), s32[]{:S(2)}) async-start(), calls=%async_computation.15 | async-start | bytes 14155776 | tf_op jit(solution)/shard_map/reduce_scatter | solution.py:273
  478.3 1.6 copy-start.11
  478.3 290.9 %reduce-scatter.16.cloned.1.call-start = ((), (), s32[]{:S(2)}) async-start(), calls=%async_computation.16 | async-start | bytes 4718592 | tf_op jit(solution)/shard_map/reduce_scatter | solution.py:275
  483.2 406.1 %reduce-scatter.18.cloned.1.call-start = ((), (), s32[]{:S(2)}) async-start(), calls=%async_computation.17 | async-start | bytes 18874368 | tf_op jit(solution)/shard_map/reduce_scatter | solution.py:276
  496.1 513.3 %reduce-scatter.20.cloned.1.call-start = ((), (), s32[]{:S(2)}) async-start(), calls=%async_computation.18 | async-start | bytes 18874368 | tf_op jit(solution)/shard_map/reduce_scatter | solution.py:278
  508.0 0.7 copy-start.35
  508.0 1.9 copy-start.27
  508.0 1.9 copy-start.28
  508.0 28.7 %copy-start.1 = (bf16[128,2048]{1,0:T(8,128)(2,1)S(1)}, bf16[128,2048]{1,0:T(8,128)(2,1)}, u32[]{:S(2)}) copy-start(bf16[128,2048]{1,0:T(8,128)(2,1)} %param.15) | copy-start | bytes 1572868
  508.0 28.7 %copy-start.17 = (f32[2048]{0:T(1024)S(1)}, f32[2048]{0:T(1024)}, u32[]{:S(2)}) copy-start(f32[2048]{0:T(1024)} %copy-done.16) | copy-start | bytes 24580
  508.0 28.7 %copy-start.23 = (f32[128]{0:T(128)S(1)}, f32[128]{0:T(128)}, u32[]{:S(2)}) copy-start(f32[128]{0:T(128)} %copy-done.22) | copy-start | bytes 1540
  508.0 30.2 %copy-start.32 = (f32[128]{0:T(128)S(1)}, f32[128]{0:T(128)}, u32[]{:S(2)}) copy-start(f32[128]{0:T(128)} %copy-done.31) | copy-start | bytes 1540
  508.0 30.2 %copy-start.26 = (f32[128]{0:T(128)S(1)}, f32[128]{0:T(128)}, u32[]{:S(2)}) copy-start(f32[128]{0:T(128)} %copy-done.25) | copy-start | bytes 1540
  508.1 108.2 %copy-start.12 = (bf16[128,2048]{1,0:T(8,128)(2,1)S(1)}, bf16[128,2048]{1,0:T(8,128)(2,1)}, u32[]{:S(2)}) copy-start(bf16[128,2048]{1,0:T(8,128)(2,1)} %param.26) | copy-start | bytes 1572868
  660.7 349.2 %copy-start.36 = (f32[64]{0:T(128)}, f32[64]{0:T(128)S(1)}, u32[]{:S(2)}) copy-start(f32[64]{0:T(128)S(1)} %dynamic-slice.2) | copy-start | bytes 772
Sparse Core Ops, SparseCore 0:
  58.4 46.3 all-gather.8
  107.2 45.3 all-gather.10
  154.2 45.9 all-gather.18
  201.9 26.8 all-gather.12
  230.6 64.4 all-gather.14
  296.8 123.3 all-gather.16
  423.8 33.6 reduce-scatter.21
  459.9 76.7 reduce-scatter.11
  539.0 77.2 reduce-scatter.9
  620.0 93.4 reduce-scatter.13
  717.9 51.3 reduce-scatter.15
  773.2 115.9 reduce-scatter.17
  893.4 115.9 reduce-scatter.19
where the time goes:
time: 1020 us
  waiting for transfers between devices  607 us (60%)
  matrix products  158 us (15%)
  blocking collectives  116 us (11%)
  other arithmetic  54 us (5%)
  local copies, waits for them, and re-layouts  40 us (4%)
  starting transfers between devices  27.1 us (3%)
  between operations  15.8 us (2%)
    reduce_scatter x1, waiting for transfers between devices, body(): lax.psum_scatter(outer_grad, 'fsdp', scatter_dimension=1, tiled=True)  120 us
    reduce_scatter x1, waiting for transfers between devices, body(): lax.psum_scatter(inner_grad, 'fsdp', scatter_dimension=0, tiled=True)  120 us
    unnamed x3, blocking collectives  97.5 us
    reduce_scatter x1, waiting for transfers between devices, body(): lax.psum_scatter(partial_rows, 'tp', scatter_dimension=0, tiled=True)  76.3 us
    reduce_scatter x1, waiting for transfers between devices, body(): lax.psum_scatter(dense_grad, 'fsdp', scatter_dimension=1, tiled=True)  52.6 us
    reduce_scatter x1, waiting for transfers between devices, body(): lax.psum_scatter(qkv_weight_part, 'fsdp', scatter_dimension=1, tiled=True)  51.6 us
    all_gather x1, waiting for transfers between devices, forward_pieces(): lax.all_gather(qkv_weight, 'fsdp', axis=1, tiled=True)  47.9 us
    ppermute x8, waiting for transfers between devices, passed_along(): lax.ppermute(value, axis, [(source, source + steps) for source in range(i...  34.4 us
  transfers between devices with their start and end apart: 21, of which 13 were waited for; matrix products, arithmetic and copies ran while one was open for 23% of the time, Pallas kernels for 0%

commit v1 on v0

--- a/solution.py
+++ b/solution.py
@@ -7,6 +7,22 @@
 ROTARY = 32
 TREE_LEN = 1024
 EPSILON = 1e-05
+
+
+def ring_gather(x, axis, dim):
+    ways, here, step = (lax.axis_size(axis), lax.axis_index(axis), x.shape[dim])
+    shape = [n * ways if d == dim else n for d, n in enumerate(x.shape)]
+    full = lax.dynamic_update_slice_in_dim(jnp.zeros(shape, x.dtype), x, here * step, axis=dim)
+    going_up = going_down = x
+    for far in range(1, ways // 2 + 1):
+        going_up = lax.ppermute(going_up, axis, [(d, (d + 1) % ways) for d in range(ways)])
+        full = lax.dynamic_update_slice_in_dim(full, going_up, (here - far) % ways * step, axis=dim)
+        if 2 * far < ways:
+            going_down = lax.ppermute(going_down, axis, [(d, (d - 1) % ways) for d in range(ways)])
+            full = lax.dynamic_update_slice_in_dim(
+                full, going_down, (here + far) % ways * step, axis=dim
+            )
+    return full
 
 
 def passed_along(value, axis, steps):
@@ -126,7 +142,7 @@
 
     def forward_pieces():
         gathered = (
-            lax.all_gather(qkv_weight, "fsdp", axis=1, tiled=True),
+            ring_gather(qkv_weight, "fsdp", 1),
             lax.all_gather(qkv_bias, "fsdp", axis=1, tiled=True),
             lax.all_gather(dense_weight, "fsdp", axis=1, tiled=True),
             lax.all_gather(inner_weight, "fsdp", axis=0, tiled=True),

time: 1020 us -> 965 us (0.946)
  waiting for transfers between devices: 607 us -> 522 us
  blocking collectives: 116 us -> 133 us
    all_gather x1 -> x0, waiting for transfers between devices: 47.9 us -> none  [forward_pieces(): lax.all_gather(qkv_weight, 'fsdp', axis=1, tiled=True)]
    all_gather x1, waiting for transfers between devices: 32.8 us -> 0.02 us  [body(): grad_rows = lax.all_gather(cotangent, 'tp', axis=0, tiled=True)]
    ppermute x0 -> x7, waiting for transfers between devices: none -> 31.7 us  [the longest x4 31.6 us: ring_gather(): lax.ppermute(going_up, axis, [(d, (d + 1) % ways) for d in range(ways)])]
    all_gather x1, waiting for transfers between devices: 28.7 us -> 0.02 us  [forward_pieces(): lax.all_gather(dense_weight, 'fsdp', axis=1, tiled=True)]
    all_gather x1, waiting for transfers between devices: 19.4 us -> 0.01 us  [forward_pieces(): normed = lax.all_gather(normed_local, 'tp', axis=0, tiled=True)]
    all_gather x1, blocking collectives: 10.2 us -> 20.7 us  [forward_pieces(): lax.all_gather(qkv_bias, 'fsdp', axis=1, tiled=True)]
    unnamed x97 -> x98, local copies, waits for them, and re-layouts: 23.9 us -> 20.3 us
  transfers between devices with their start and end apart: 21 -> 27, of which waited for: 13 -> 13; matrix products, arithmetic and copies ran while one was open for 23% -> 25% of each run, Pallas kernels for 0% -> 0%
where the time goes in v1:
time: 965 us; the launch traced here: 956 us
  waiting for transfers between devices  522 us (54%)
  matrix products  160 us (17%)
  blocking collectives  133 us (14%)
  other arithmetic  54.1 us (6%)
  local copies, waits for them, and re-layouts  47.1 us (5%)
  starting transfers between devices  24.9 us (3%)
  between operations  16.1 us (2%)
    reduce_scatter x1, waiting for transfers between devices, body(): lax.psum_scatter(inner_grad, 'fsdp', scatter_dimension=0, tiled=True)  120 us
    reduce_scatter x1, waiting for transfers between devices, body(): lax.psum_scatter(outer_grad, 'fsdp', scatter_dimension=1, tiled=True)  120 us
    unnamed x3, blocking collectives  97.5 us
    reduce_scatter x1, waiting for transfers between devices, body(): lax.psum_scatter(partial_rows, 'tp', scatter_dimension=0, tiled=True)  76.3 us
    reduce_scatter x1, waiting for transfers between devices, body(): lax.psum_scatter(dense_grad, 'fsdp', scatter_dimension=1, tiled=True)  52.5 us
    reduce_scatter x1, waiting for transfers between devices, body(): lax.psum_scatter(qkv_weight_part, 'fsdp', scatter_dimension=1, tiled=True)  51.8 us
    ppermute x8, waiting for transfers between devices, passed_along(): lax.ppermute(value, axis, [(source, source + steps) for source in range(i...  40.7 us
    ppermute x4, waiting for transfers between devices, ring_gather(): lax.ppermute(going_up, axis, [(d, (d + 1) % ways) for d in range(ways)])  31.6 us
  transfers between devices with their start and end apart: 27, of which 13 were waited for; matrix products, arithmetic and copies ran while one was open for 25% of the time, Pallas kernels for 0%

profile of v1, /device:TPU:0, one launch (start us, length us, event | category | flops | bytes accessed | tf_op | source)
XLA Modules:
  0.0 956.4 jit_solution(10730499948898639781)
XLA Ops:
  10.8 42.2 %all-reduce.11 = (bf16[2048]{0:T(1024)(128)(2,1)S(1)}, bf16[2048]{0:T(1024)(128)(2,1)S(1)}, bf16[2048]{0:T(1024)(128)(2,1)}, bf16[2048]{0:T(1024)(128)(2,1)}) all-reduce(bf16[2048]{0:T(1024)(128)(2,1)S(1)} %dynamic-update-slice.1, bf16[2048]{0:T(1024)(128)(2,1)S(1)} %dynamic-update-slice, ...), channel_id=1, replica_groups=mesh['fsdp'=8,'tp'=4] {'fsdp','tp'}, use_global_device_ids=true, to_apply=%add.3 | all-reduce | flops 8192 | bytes 32768
  55.6 2.2 fusion.31
  60.0 2.6 collective-permute-start.1
  62.7 20.7 %all-gather = bf16[8,64,3]{1,2,0:T(4,128)(2,1)S(1)} all-gather(bf16[1,64,3]{1,2,0:T(4,128)(2,1)S(1)} %bitcast.110), channel_id=1, replica_groups=mesh['fsdp'=8,'tp'=4] {'fsdp'}, dimensions={0}, use_global_device_ids=true | all-gather | bytes 3456 | tf_op jit(solution)/shard_map/all_gather | solution.py:146
  84.3 1.9 convert_reduce_fusion.2
  86.2 2.4 collective-permute-start.3
  88.5 13.9 %collective-permute-done.2 = bf16[3,256,512]{2,1,0:T(8,128)(2,1)S(1)} collective-permute-done((bf16[3,256,512]{2,1,0:T(8,128)(2,1)S(1)}, bf16[3,256,512]{2,1,0:T(8,128)(2,1)S(1)}, u32[]{:S(2)}, u32[]{:S(2)}) %collective-permute-start.2) | collective-permute-done | bytes 786464 | tf_op jit(solution)/shard_map/ppermute | solution.py:18
  103.5 2.8 collective-permute-start.5
  106.3 3.1 broadcast.347
  110.3 11.0 %collective-permute-done.4 = bf16[3,256,512]{2,1,0:T(8,128)(2,1)S(1)} collective-permute-done((bf16[3,256,512]{2,1,0:T(8,128)(2,1)S(1)}, bf16[3,256,512]{2,1,0:T(8,128)(2,1)S(1)}, u32[]{:S(2)}, u32[]{:S(2)}) %collective-permute-start.4) | collective-permute-done | bytes 786464 | tf_op jit(solution)/shard_map/ppermute | solution.py:18
  127.1 6.6 collective-permute-done.6
  134.7 6.3 add_bitcast_fusion
  142.6 2.1 collective-permute-start.9
  144.7 2.1 collective-permute-start.10
  146.9 14.4 %all-gather.1 = bf16[8,1,256]{2,1,0:T(2,128)(2,1)S(1)} all-gather(bf16[1,1,256]{2,1,0:T(2,128)(2,1)S(1)} %reshape.435), channel_id=1, replica_groups=mesh['fsdp'=8,'tp'=4] {'fsdp'}, dimensions={0}, use_global_device_ids=true | all-gather | bytes 4608 | tf_op jit(solution)/shard_map/all_gather | solution.py:149
  163.2 4.0 collective-permute-start.7
  167.2 2.1 collective-permute-start.8
  169.4 12.0 %select_reduce_fusion = (f32[8,512]{1,0:T(8,128)S(1)}, f32[8,512,1536]{2,1,0:T(8,128)}) fusion(pred[512,1536]{1,0:T(8,128)(4,1)S(1)} %get-tuple-element.236, bf16[512,8,64]{0,2,1:T(8,128)(2,1)S(1)} %maximum_convert_fusion, bf16[512,8,64]{0,2,1:T(8,128)(2,1)} %bitcast.14, bf16[512,8,64]{0,2,1:T(8,128)(2,1)} %bitcast.13, bf16[512,8,32]{0,2,1:T(8,128)(2,1)S(1)} %slice.202, ...), kind=kOutput, calls=%fused_computation.5 | convolution fusion | flops 830468096 | bytes 28065792 | tf_op jit(solution)/shard_map/while/body/eval_jaxpr/qhe,khe->hqk/dot_general | solution.py:173
  181.4 11.6 %fusion = f32[8,512]{1,0:T(8,128)S(1)} fusion(f32[8,512,1536]{2,1,0:T(8,128)} %get-tuple-element.268, f32[8,512]{1,0:T(8,128)S(1)} %get-tuple-element.267, pred[512,1536]{1,0:T(8,128)(4,1)S(1)} %get-tuple-element.236), kind=kLoop, calls=%fused_computation.6 | loop fusion | flops 25161728 | bytes 25985024 | tf_op jit(solution)/shard_map/while/body/eval_jaxpr/reduce_sum | solution.py:178
  193.2 4.0 convolution_convert_fusion
  197.2 20.0 %multiply_reduce_fusion = (f32[8,512]{1,0:T(8,128)S(1)}, f32[8,512,1536]{2,1,0:T(8,128)}) fusion(f32[8,512,1536]{2,1,0:T(8,128)} %get-tuple-element.268, f32[8,512]{1,0:T(8,128)S(1)} %log_add_fusion, pred[512,1536]{1,0:T(8,128)(4,1)S(1)} %get-tuple-element.236, bf16[512,8,64]{0,2,1:T(8,128)(2,1)S(1)} %bitcast.100, bf16[1536,8,64]{0,2,1:T(8,128)(2,1)S(1)} %bitcast.82), kind=kOutput, calls=%fused_computation.1 | convolution fusion | flops 836759552 | bytes 53248000 | tf_op jit(solution)/shard_map/while/body/eval_jaxpr/qhe,khe->hqk/dot_general | solution.py:238
  217.2 17.4 %multiply_convert_fusion = bf16[8,512,1536]{2,1,0:T(8,128)(2,1)S(1)} fusion(f32[8,512,1536]{2,1,0:T(8,128)} %get-tuple-element.270, f32[8,512,1536]{2,1,0:T(8,128)} %get-tuple-element.268, f32[8,512]{1,0:T(8,128)S(1)} %get-tuple-element.269, f32[8,512]{1,0:T(8,128)S(1)} %log_add_fusion, pred[512,1536]{1,0:T(8,128)(4,1)S(1)} %get-tuple-element.236), kind=kLoop, calls=%fused_computation | loop fusion | flops 37748736 | bytes 63733760 | tf_op jit(solution)/shard_map/while/body/eval_jaxpr/convert_element_type | solution.py:240
  234.6 2.3 fusion.13
  236.9 2.2 copy-done
  239.2 1.7 fusion.57
  242.2 1.7 collective-permute-start.12
  243.9 11.8 %fusion.14 = f32[1536,8,64]{0,2,1:T(8,128)S(1)} fusion(bf16[512,8,64]{0,2,1:T(8,128)(2,1)S(1)} %bitcast.101, f32[8,512,1536]{2,1,0:T(8,128)} %get-tuple-element.268, f32[8,512]{1,0:T(8,128)S(1)} %log_add_fusion, pred[512,1536]{1,0:T(8,128)(4,1)S(1)} %get-tuple-element.236), kind=kOutput, calls=%fused_computation.26 | convolution fusion | flops 830472192 | bytes 29638656 | tf_op jit(solution)/shard_map/while/body/eval_jaxpr/hqk,qhe->khe/dot_general | solution.py:248
  255.7 1.6 fusion.58
  257.3 2.5 copy.67
  263.7 9.0 fusion.26
  273.7 1.6 copy.68
  275.3 28.1 %collective-permute-done.12 = f32[512,512]{0,1:T(8,128)} collective-permute-done((f32[512,512]{0,1:T(8,128)}, f32[512,512]{0,1:T(8,128)}, u32[]{:S(2)}, u32[]{:S(2)}) %collective-permute-start.12) | collective-permute-done | bytes 1048608 | tf_op jit(solution)/shard_map/ppermute | solution.py:31
  303.4 2.2 fusion.38
  306.4 1.6 subtract_convert_fusion.1
  308.8 2.0 copy.70
  310.9 1.8 pad_maximum_fusion.7
  312.7 2.0 copy.71
  314.7 12.6 %collective-permute-done.14 = f32[512,512]{1,0:T(8,128)} collective-permute-done((f32[512,512]{1,0:T(8,128)}, f32[512,512]{1,0:T(8,128)}, u32[]{:S(2)}, u32[]{:S(2)}) %collective-permute-start.14) | collective-permute-done | bytes 1048608 | tf_op jit(solution)/shard_map/ppermute | solution.py:31
  327.3 1.8 fusion.40
  332.5 10.9 %fusion.61 = f32[512,2048]{1,0:T(8,128)} fusion(bf16[512,2048]{1,0:T(8,128)(2,1)} %all-gather.8.cloned.1.call-done, bf16[2048,2048]{1,0:T(8,128)(2,1)} %all-gather.12.cloned.1.call-done), kind=kOutput, calls=%fused_computation.131 | convolution fusion | flops 4294967296 | bytes 14680064 | tf_op jit(solution)/shard_map/dot_general | solution.py:185
  343.5 16.1 %all-gather.14.cloned.1.call-done = bf16[2048,2048]{1,0:T(8,128)(2,1)} async-done(((bf16[2048,256]{1,0:T(8,128)(2,1)}), bf16[2048,2048]{1,0:T(8,128)(2,1)}) %all-gather.14.cloned.1.call-update) | async-done | bytes 8388624 | tf_op jit(solution)/shard_map/all_gather | solution.py:150
  359.6 12.2 %convert_reduce_fusion = (f32[2048]{0:T(1024)S(1)}, bf16[512,2048]{1,0:T(8,128)(2,1)S(1)}) fusion(f32[512,2048]{1,0:T(8,128)} %fusion.61, f32[2048]{0:T(1024)S(1)} %bitcast.106, bf16[512,2048]{1,0:T(8,128)(2,1)} %all-gather.16.cloned.1.call-done, bf16[2048,2048]{1,0:T(8,128)(2,1)} %all-gather.14.cloned.1.call-done), kind=kOutput, calls=%fused_computation.22 | convolution fusion | flops 4319082496 | bytes 16793600 | tf_op jit(solution)/shard_map/td,fd->tf/dot_general | solution.py:217
  371.9 4.8 fusion.62
  376.7 7.9 bitcast_add_fusion
  385.3 11.6 %fusion.27 = bf16[8,64,512]{2,1,0:T(8,128)(2,1)S(1)} fusion(bf16[1536,8,64]{0,2,1:T(8,128)(2,1)S(1)} %bitcast.83, f32[8,512,1536]{2,1,0:T(8,128)} %get-tuple-element.268, f32[8,512]{1,0:T(8,128)S(1)} %copy-done.20, f32[8,512]{1,0:T(8,128)S(1)} %get-tuple-element.267, pred[512,1536]{1,0:T(8,128)(4,1)S(1)} %get-tuple-element.236), kind=kOutput, calls=%fused_computation.51 | convolution fusion | flops 837025792 | bytes 28082176 | tf_op jit(solution)/shard_map/while/body/eval_jaxpr/hqk,khe->qhe/dot_general | solution.py:180
  397.0 8.1 fusion.54
  405.1 3.4 convolution_add_fusion
  409.7 7.9 convolution_bitcast_fusion
  417.7 1.5 copy-done.11
  419.2 3.2 fusion.63
  422.8 12.5 %fusion.64 = f32[2048,2048]{1,0:T(8,128)} fusion(bf16[512,2048]{1,0:T(8,128)(2,1)} %all-gather.8.cloned.1.call-done, bf16[512,2048]{1,0:T(8,128)(2,1)} %copy-done.38), kind=kOutput, calls=%fused_computation.134 | convolution fusion | flops 4294967296 | bytes 20971520 | tf_op jit(solution)/shard_map/td,tf->df/dot_general | solution.py:222
  435.4 12.1 %fusion.53 = f32[2048,2048]{1,0:T(8,128)} fusion(bf16[512,2048]{1,0:T(8,128)(2,1)S(1)} %copy-done.11, f32[512,2048]{1,0:T(8,128)} %fusion.61, f32[2048]{0:T(1024)S(1)} %bitcast.108), kind=kOutput, calls=%fused_computation.124 | convolution fusion | flops 4305453056 | bytes 23076864 | tf_op jit(solution)/shard_map/tf,td->fd/dot_general | solution.py:216
  450.9 14.1 %all-reduce.9 = f32[2048]{0:T(1024)S(1)} all-reduce(f32[2048]{0:T(1024)S(1)} %get-tuple-element.233), channel_id=11, replica_groups=mesh['fsdp'=8,'tp'=4] {'fsdp'}, use_global_device_ids=true, to_apply=%region_23.24.clone | all-reduce | flops 2048 | bytes 16384
  465.6 10.3 %reduce-scatter.12.cloned.1.call-done = f32[128,2048]{1,0:T(8,128)} async-done(((f32[512,2048]{1,0:T(8,128)}), f32[128,2048]{1,0:T(8,128)}) %reduce-scatter.12.cloned.1.call-update) | async-done | bytes 1048592 | tf_op jit(solution)/shard_map/reduce_scatter | solution.py:284
  475.9 1.6 fusion.55
  477.5 1.7 fusion.32
  479.3 76.3 %reduce-scatter.10.cloned.1.call-done = f32[128,2048]{1,0:T(8,128)} async-done(((f32[512,2048]{1,0:T(8,128)}), f32[128,2048]{1,0:T(8,128)}) %reduce-scatter.10.cloned.1.call-update) | async-done | bytes 1048592 | tf_op jit(solution)/shard_map/reduce_scatter | solution.py:205
  555.5 3.2 convert_reduce_fusion.4
  558.7 41.2 %all-reduce.10 = (f32[2048]{0:T(1024)S(1)}, f32[2048]{0:T(1024)S(1)}, f32[2048]{0:T(1024)S(1)}) all-reduce(f32[2048]{0:T(1024)S(1)} %get-tuple-element.222, f32[2048]{0:T(1024)S(1)} %get-tuple-element.224, f32[2048]{0:T(1024)S(1)} %get-tuple-element.253), channel_id=4, replica_groups=mesh['fsdp'=8,'tp'=4] {'fsdp','tp'}, use_global_device_ids=true, to_apply=%region_12.13.clone | all-reduce | flops 6144 | bytes 49152
  601.2 51.8 %reduce-scatter.14.cloned.1.call-done = f32[3,256,512]{1,2,0:T(8,128)} async-done(((f32[3,2048,512]{1,2,0:T(8,128)}), f32[3,256,512]{1,2,0:T(8,128)}) %reduce-scatter.14.cloned.1.call-update) | async-done | bytes 1572880 | tf_op jit(solution)/shard_map/reduce_scatter | solution.py:289
  653.0 3.0 copy.73
  656.0 52.5 %reduce-scatter.16.cloned.1.call-done = f32[512,256]{1,0:T(8,128)} async-done(((f32[512,2048]{1,0:T(8,128)}), f32[512,256]{1,0:T(8,128)}) %reduce-scatter.16.cloned.1.call-update) | async-done | bytes 524304 | tf_op jit(solution)/shard_map/reduce_scatter | solution.py:291
  708.5 120.1 %reduce-scatter.18.cloned.1.call-done = f32[256,2048]{1,0:T(8,128)} async-done(((f32[2048,2048]{1,0:T(8,128)}), f32[256,2048]{1,0:T(8,128)}) %reduce-scatter.18.cloned.1.call-update) | async-done | bytes 2097168 | tf_op jit(solution)/shard_map/reduce_scatter | solution.py:292
  828.6 120.0 %reduce-scatter.20.cloned.1.call-done = f32[2048,256]{1,0:T(8,128)} async-done(((f32[2048,2048]{1,0:T(8,128)}), f32[2048,256]{1,0:T(8,128)}) %reduce-scatter.20.cloned.1.call-update) | async-done | bytes 2097168 | tf_op jit(solution)/shard_map/reduce_scatter | solution.py:294
  (187 shorter events, 40.1 us)
Async XLA Ops:
  7.2 52.8 %copy-start.16 = (bf16[3,256,512]{2,1,0:T(8,128)(2,1)S(1)}, bf16[3,256,512]{2,1,0:T(8,128)(2,1)}, u32[]{:S(2)}) copy-start(bf16[3,256,512]{2,1,0:T(8,128)(2,1)} %param.18) | copy-start | bytes 2359300
  7.2 55.5 %copy-start.31 = (bf16[3,64]{1,0:T(4,128)(2,1)S(1)}, bf16[3,64]{1,0:T(4,128)(2,1)}, u32[]{:S(2)}) copy-start(bf16[3,64]{1,0:T(4,128)(2,1)} %param.19) | copy-start | bytes 1156
  7.2 76.3 %copy-start.22 = (s32[4096]{0:T(1024)S(1)}, s32[4096]{0:T(1024)}, u32[]{:S(2)}) copy-start(s32[4096]{0:T(1024)} %param.27) | copy-start | bytes 49156
  7.2 76.3 %copy-start.21 = (s32[4096]{0:T(1024)S(1)}, s32[4096]{0:T(1024)}, u32[]{:S(2)}) copy-start(s32[4096]{0:T(1024)} %param.29) | copy-start | bytes 49156
  7.2 76.5 %copy-start.30 = (s32[39,3]{0,1:T(4,128)S(1)}, s32[39,3]{0,1:T(4,128)}, u32[]{:S(2)}) copy-start(s32[39,3]{0,1:T(4,128)} %param.28) | copy-start | bytes 1408
  7.2 127.4 %all-gather.8.cloned.1.call-start = ((), (), s32[]{:S(2)}) async-start(), calls=%async_computation.7 | async-start | bytes 2621440 | tf_op jit(solution)/shard_map/all_gather | solution.py:152
  53.0 2.6 copy-start.17
  54.2 30.1 %copy-start.23 = (f32[128]{0:T(128)}, f32[128]{0:T(128)S(1)}, u32[]{:S(2)}) copy-start(f32[128]{0:T(128)S(1)} %broadcast_multiply_fusion.1) | copy-start | bytes 1540
  55.5 28.7 %copy-start.32 = (f32[128]{0:T(128)}, f32[128]{0:T(128)S(1)}, u32[]{:S(2)}) copy-start(f32[128]{0:T(128)S(1)} %fusion.34) | copy-start | bytes 1540
  55.6 28.7 %copy-start.26 = (f32[128]{0:T(128)}, f32[128]{0:T(128)S(1)}, u32[]{:S(2)}) copy-start(f32[128]{0:T(128)S(1)} %fusion.44) | copy-start | bytes 1540
  57.8 135.4 %all-gather.16.cloned.1.call-start = ((), (), s32[]{:S(2)}) async-start(), calls=%async_computation.12 | async-start | bytes 2621440 | tf_op jit(solution)/shard_map/all_gather | solution.py:208
  58.6 134.6 %all-gather.10.cloned.1.call-start = ((), (), s32[]{:S(2)}) async-start(), calls=%async_computation.8 | async-start | bytes 2359296 | tf_op jit(solution)/shard_map/all_gather | solution.py:147
  59.3 273.2 %all-gather.12.cloned.1.call-start = ((), (), s32[]{:S(2)}) async-start(), calls=%async_computation.9 | async-start | bytes 9437184 | tf_op jit(solution)/shard_map/all_gather | solution.py:148
  59.9 299.7 %all-gather.14.cloned.1.call-start = ((), (), s32[]{:S(2)}) async-start(), calls=%async_computation.10 | async-start | bytes 9437184 | tf_op jit(solution)/shard_map/all_gather | solution.py:150
  60.0 24.0 %collective-permute-start = (bf16[3,256,512]{2,1,0:T(8,128)(2,1)S(1)}, bf16[3,256,512]{2,1,0:T(8,128)(2,1)S(1)}, u32[]{:S(2)}, u32[]{:S(2)}) collective-permute-start(bf16[3,256,512]{2,1,0:T(8,128)(2,1)S(1)} %copy-done.16), channel_id=1, source_target_pairs={{0,4},{4,8},{8,12},{12,16},{16,20},{20,24},{24,28},{28,0},{1,5},{5... | collective-permute-start | bytes 2359304 | tf_op jit(solution)/shard_map/ppermute | solution.py:18
  60.0 26.1 %collective-permute-start.1 = (bf16[3,256,512]{2,1,0:T(8,128)(2,1)S(1)}, bf16[3,256,512]{2,1,0:T(8,128)(2,1)S(1)}, u32[]{:S(2)}, u32[]{:S(2)}) collective-permute-start(bf16[3,256,512]{2,1,0:T(8,128)(2,1)S(1)} %copy-done.16), channel_id=1, source_target_pairs={{0,28},{4,0},{8,4},{12,8},{16,12},{20,16},{24,20},{28,24},{1,29},{... | collective-permute-start | bytes 2359304 | tf_op jit(solution)/shard_map/ppermute | solution.py:21
  83.9 18.5 %collective-permute-start.2 = (bf16[3,256,512]{2,1,0:T(8,128)(2,1)S(1)}, bf16[3,256,512]{2,1,0:T(8,128)(2,1)S(1)}, u32[]{:S(2)}, u32[]{:S(2)}) collective-permute-start(bf16[3,256,512]{2,1,0:T(8,128)(2,1)S(1)} %collective-permute-done), channel_id=1, source_target_pairs={{0,4},{4,8},{8,12},{12,16},{16,20},{20,24},{24,28},{28,0},{1,5},{5... | collective-permute-start | bytes 2359304 | tf_op jit(solution)/shard_map/ppermute | solution.py:18
  86.2 17.3 %collective-permute-start.3 = (bf16[3,256,512]{2,1,0:T(8,128)(2,1)S(1)}, bf16[3,256,512]{2,1,0:T(8,128)(2,1)S(1)}, u32[]{:S(2)}, u32[]{:S(2)}) collective-permute-start(bf16[3,256,512]{2,1,0:T(8,128)(2,1)S(1)} %collective-permute-done.1), channel_id=1, source_target_pairs={{0,28},{4,0},{8,4},{12,8},{16,12},{20,16},{24,20},{28,24},{1,29},{... | collective-permute-start | bytes 2359304 | tf_op jit(solution)/shard_map/ppermute | solution.py:21
  102.4 18.9 %collective-permute-start.4 = (bf16[3,256,512]{2,1,0:T(8,128)(2,1)S(1)}, bf16[3,256,512]{2,1,0:T(8,128)(2,1)S(1)}, u32[]{:S(2)}, u32[]{:S(2)}) collective-permute-start(bf16[3,256,512]{2,1,0:T(8,128)(2,1)S(1)} %collective-permute-done.2), channel_id=1, source_target_pairs={{0,4},{4,8},{8,12},{12,16},{16,20},{20,24},{24,28},{28,0},{1,5},{5... | collective-permute-start | bytes 2359304 | tf_op jit(solution)/shard_map/ppermute | solution.py:18
  103.5 22.6 %collective-permute-start.5 = (bf16[3,256,512]{2,1,0:T(8,128)(2,1)S(1)}, bf16[3,256,512]{2,1,0:T(8,128)(2,1)S(1)}, u32[]{:S(2)}, u32[]{:S(2)}) collective-permute-start(bf16[3,256,512]{2,1,0:T(8,128)(2,1)S(1)} %collective-permute-done.3), channel_id=1, source_target_pairs={{0,28},{4,0},{8,4},{12,8},{16,12},{20,16},{24,20},{28,24},{1,29},{... | collective-permute-start | bytes 2359304 | tf_op jit(solution)/shard_map/ppermute | solution.py:21
  121.4 12.3 %collective-permute-start.6 = (bf16[3,256,512]{2,1,0:T(8,128)(2,1)S(1)}, bf16[3,256,512]{2,1,0:T(8,128)(2,1)S(1)}, u32[]{:S(2)}, u32[]{:S(2)}) collective-permute-start(bf16[3,256,512]{2,1,0:T(8,128)(2,1)S(1)} %collective-permute-done.4), channel_id=1, source_target_pairs={{0,4},{4,8},{8,12},{12,16},{16,20},{20,24},{24,28},{28,0},{1,5},{5... | collective-permute-start | bytes 2359304 | tf_op jit(solution)/shard_map/ppermute | solution.py:18
  140.9 1.6 copy-start.4
  140.9 6.0 copy-start.35
  142.6 38.8 %copy-start.14 = (bf16[512,8,64]{0,2,1:T(8,128)(2,1)}, bf16[512,8,64]{0,2,1:T(8,128)(2,1)S(1)}, u32[]{:S(2)}) copy-start(bf16[512,8,64]{0,2,1:T(8,128)(2,1)S(1)} %maximum_convert_fusion) | copy-start | bytes 1572868
  142.6 26.8 %collective-permute-start.9 = (bf16[512,512]{0,1:T(8,128)(2,1)S(1)}, bf16[512,512]{0,1:T(8,128)(2,1)}, u32[]{:S(2)}, u32[]{:S(2)}) collective-permute-start(bf16[512,512]{0,1:T(8,128)(2,1)S(1)} %bitcast.97), channel_id=1, source_target_pairs={{0,8},{4,12},{8,16},{12,20},{16,24},{20,28},{1,9},{5,13},{9,17},{1... | collective-permute-start | bytes 1572872 | tf_op jit(solution)/shard_map/ppermute | solution.py:31
  144.7 24.7 %collective-permute-start.10 = (bf16[512,512]{0,1:T(8,128)(2,1)S(1)}, bf16[512,512]{0,1:T(8,128)(2,1)}, u32[]{:S(2)}, u32[]{:S(2)}) collective-permute-start(bf16[512,512]{0,1:T(8,128)(2,1)S(1)} %bitcast.98), channel_id=1, source_target_pairs={{0,4},{4,8},{8,12},{12,16},{16,20},{20,24},{24,28},{1,5},{5,9},{9,... | collective-permute-start | bytes 1572872 | tf_op jit(solution)/shard_map/ppermute | solution.py:31
  146.9 302.6 %reduce-scatter.22.cloned.1.call-start = ((), (), s32[]{:S(2)}) async-start(), calls=%async_computation.18 | async-start | bytes 294912
  163.2 29.9 %collective-permute-start.7 = (bf16[512,512]{0,1:T(8,128)(2,1)S(1)}, bf16[512,512]{0,1:T(8,128)(2,1)S(1)}, u32[]{:S(2)}, u32[]{:S(2)}) collective-permute-start(bf16[512,512]{0,1:T(8,128)(2,1)S(1)} %fusion.41), channel_id=1, source_target_pairs={{0,8},{4,12},{8,16},{12,20},{16,24},{20,28},{1,9},{5,13},{9,17},{1... | collective-permute-start | bytes 1572872 | tf_op jit(solution)/shard_map/ppermute | solution.py:31
  167.2 25.9 %collective-permute-start.8 = (bf16[512,512]{0,1:T(8,128)(2,1)S(1)}, bf16[512,512]{0,1:T(8,128)(2,1)S(1)}, u32[]{:S(2)}, u32[]{:S(2)}) collective-permute-start(bf16[512,512]{0,1:T(8,128)(2,1)S(1)} %fusion.41), channel_id=1, source_target_pairs={{0,4},{4,8},{8,12},{12,16},{16,20},{20,24},{24,28},{1,5},{5,9},{9,... | collective-permute-start | bytes 1572872 | tf_op jit(solution)/shard_map/ppermute | solution.py:31
  193.0 4.2 copy-start.19
  234.6 4.5 copy-start
  240.9 34.4 %collective-permute-start.11 = (f32[512,512]{0,1:T(8,128)}, f32[512,512]{0,1:T(8,128)}, u32[]{:S(2)}, u32[]{:S(2)}) collective-permute-start(f32[512,512]{0,1:T(8,128)} %bitcast.23), channel_id=1, source_target_pairs={{4,0},{8,4},{12,8},{16,12},{20,16},{24,20},{28,24},{5,1},{9,5},{13... | collective-permute-start | bytes 3145736 | tf_op jit(solution)/shard_map/ppermute | solution.py:31
  242.2 61.2 %collective-permute-start.12 = (f32[512,512]{0,1:T(8,128)}, f32[512,512]{0,1:T(8,128)}, u32[]{:S(2)}, u32[]{:S(2)}) collective-permute-start(f32[512,512]{0,1:T(8,128)} %bitcast.24), channel_id=1, source_target_pairs={{8,0},{12,4},{16,8},{20,12},{24,16},{28,20},{9,1},{13,5},{17,9},{2... | collective-permute-start | bytes 3145736 | tf_op jit(solution)/shard_map/ppermute | solution.py:31
  259.8 54.9 %collective-permute-start.13 = (f32[512,512]{1,0:T(8,128)}, f32[512,512]{1,0:T(8,128)}, u32[]{:S(2)}, u32[]{:S(2)}) collective-permute-start(f32[512,512]{1,0:T(8,128)} %copy.67), channel_id=1, source_target_pairs={{4,0},{8,4},{12,8},{16,12},{20,16},{24,20},{28,24},{5,1},{9,5},{13... | collective-permute-start | bytes 3145736 | tf_op jit(solution)/shard_map/ppermute | solution.py:31
  262.4 64.9 %collective-permute-start.14 = (f32[512,512]{1,0:T(8,128)}, f32[512,512]{1,0:T(8,128)}, u32[]{:S(2)}, u32[]{:S(2)}) collective-permute-start(f32[512,512]{1,0:T(8,128)} %copy.69), channel_id=1, source_target_pairs={{8,0},{12,4},{16,8},{20,12},{24,16},{28,20},{9,1},{13,5},{17,9},{2... | collective-permute-start | bytes 3145736 | tf_op jit(solution)/shard_map/ppermute | solution.py:31
  272.7 1.1 copy-start.2
  275.3 31.1 %copy-start.3 = (f32[512,8,64]{0,2,1:T(8,128)S(1)}, f32[512,8,64]{0,2,1:T(8,128)}, u32[]{:S(2)}) copy-start(f32[512,8,64]{0,2,1:T(8,128)} %copy-done.2) | copy-start | bytes 3145732
  275.3 32.7 %copy-start.15 = (bf16[512,8,32]{0,2,1:T(8,128)(2,1)S(1)}, bf16[512,8,32]{0,2,1:T(8,128)(2,1)}, u32[]{:S(2)}) copy-start(bf16[512,8,32]{0,2,1:T(8,128)(2,1)} %slice.201) | copy-start | bytes 786436
  332.3 27.4 %copy-start.25 = (f32[8,1,256]{2,1,0:T(1,128)S(1)}, f32[8,1,256]{2,1,0:T(1,128)}, u32[]{:S(2)}) copy-start(f32[8,1,256]{2,1,0:T(1,128)} %convert_element_type.155) | copy-start | bytes 24580
  332.3 143.7 %reduce-scatter.12.cloned.1.call-start = ((), (), s32[]{:S(2)}) async-start(), calls=%async_computation.13 | async-start | bytes 5242880 | tf_op jit(solution)/shard_map/reduce_scatter | solution.py:284
  359.6 12.3 %copy-start.34 = (bf16[2048,2048]{1,0:T(8,128)(2,1)S(1)}, bf16[2048,2048]{1,0:T(8,128)(2,1)}, u32[]{:S(2)}) copy-start(bf16[2048,2048]{1,0:T(8,128)(2,1)} %all-gather.12.cloned.1.call-done) | copy-start | bytes 25165828
  371.9 4.8 copy-start.38
  371.9 4.8 copy-start.6
  371.9 4.8 copy-start.7
  371.9 4.8 copy-start.9
  384.6 170.9 %reduce-scatter.10.cloned.1.call-start = ((), (), s32[]{:S(2)}) async-start(), calls=%async_computation.11 | async-start | bytes 5242880 | tf_op jit(solution)/shard_map/reduce_scatter | solution.py:205
  385.3 11.6 %copy-start.39 = (f32[512,2048]{1,0:T(8,128)S(1)}, f32[512,2048]{1,0:T(8,128)}, u32[]{:S(2)}) copy-start(f32[512,2048]{1,0:T(8,128)} %fusion.61) | copy-start | bytes 12582916
  397.0 8.1 copy-start.13
  408.5 1.0 copy-start.8
  408.5 1.2 copy-start.10
  408.5 244.4 %reduce-scatter.14.cloned.1.call-start = ((), (), s32[]{:S(2)}) async-start(), calls=%async_computation.14 | async-start | bytes 14155776 | tf_op jit(solution)/shard_map/reduce_scatter | solution.py:289
  417.6 1.6 copy-start.11
  417.7 290.8 %reduce-scatter.16.cloned.1.call-start = ((), (), s32[]{:S(2)}) async-start(), calls=%async_computation.15 | async-start | bytes 4718592 | tf_op jit(solution)/shard_map/reduce_scatter | solution.py:291
  422.5 406.1 %reduce-scatter.18.cloned.1.call-start = ((), (), s32[]{:S(2)}) async-start(), calls=%async_computation.16 | async-start | bytes 18874368 | tf_op jit(solution)/shard_map/reduce_scatter | solution.py:292
  435.3 513.3 %reduce-scatter.20.cloned.1.call-start = ((), (), s32[]{:S(2)}) async-start(), calls=%async_computation.17 | async-start | bytes 18874368 | tf_op jit(solution)/shard_map/reduce_scatter | solution.py:294
  447.5 1.9 copy-start.28
  447.5 1.9 copy-start.29
  447.5 28.4 %copy-start.1 = (bf16[128,2048]{1,0:T(8,128)(2,1)S(1)}, bf16[128,2048]{1,0:T(8,128)(2,1)}, u32[]{:S(2)}) copy-start(bf16[128,2048]{1,0:T(8,128)(2,1)} %param.15) | copy-start | bytes 1572868
  447.5 28.4 %copy-start.18 = (f32[2048]{0:T(1024)S(1)}, f32[2048]{0:T(1024)}, u32[]{:S(2)}) copy-start(f32[2048]{0:T(1024)} %copy-done.17) | copy-start | bytes 24580
  447.5 28.4 %copy-start.24 = (f32[128]{0:T(128)S(1)}, f32[128]{0:T(128)}, u32[]{:S(2)}) copy-start(f32[128]{0:T(128)} %copy-done.23) | copy-start | bytes 1540
  447.5 29.9 %copy-start.33 = (f32[128]{0:T(128)S(1)}, f32[128]{0:T(128)}, u32[]{:S(2)}) copy-start(f32[128]{0:T(128)} %copy-done.32) | copy-start | bytes 1540
  447.6 30.0 %copy-start.27 = (f32[128]{0:T(128)S(1)}, f32[128]{0:T(128)}, u32[]{:S(2)}) copy-start(f32[128]{0:T(128)} %copy-done.26) | copy-start | bytes 1540
  447.6 108.0 %copy-start.12 = (bf16[128,2048]{1,0:T(8,128)(2,1)S(1)}, bf16[128,2048]{1,0:T(8,128)(2,1)}, u32[]{:S(2)}) copy-start(bf16[128,2048]{1,0:T(8,128)(2,1)} %param.26) | copy-start | bytes 1572868
  600.0 349.1 %copy-start.37 = (f32[64]{0:T(128)}, f32[64]{0:T(128)S(1)}, u32[]{:S(2)}) copy-start(f32[64]{0:T(128)S(1)} %dynamic-slice.2) | copy-start | bytes 772
  (3 other events, 2.2 us)
Sparse Core Ops, SparseCore 0:
  58.0 46.2 all-gather.7
  105.9 44.6 all-gather.15
  152.4 32.1 all-gather.9
  186.4 54.8 all-gather.11
  243.0 116.5 all-gather.13
  363.1 33.6 reduce-scatter.21
  399.1 76.7 reduce-scatter.11
  478.2 77.2 reduce-scatter.9
  559.4 93.4 reduce-scatter.13
  657.1 51.3 reduce-scatter.15
  712.6 115.9 reduce-scatter.17
  832.6 115.9 reduce-scatter.19
